TPU v7x, 32 devices: a whole 2x2x4 slice. The times are simulated.
32 devices in a mesh: seq: 8 (over z, y), batch: 4 (over x, core).
Axes of the slice: x: 2, y: 2, z: 4, core: 2. Of those that a mesh axis runs over, the one named last changes fastest.
Arguments:
- signal: bfloat16 [4, 1024, 8192], P('batch', 'seq'), may hold values from -6 to 6
- out_grad: bfloat16 [4, 1024, 8192], P('batch', 'seq'), may hold values from -6 to 6
- residues: float32 [8, 8192], replicated, may hold values from -0.3 to 0.3
- log_rates: float32 [8, 512], replicated, as said below
Outputs:
- mixed: bfloat16 [4, 1024, 8192], P('batch', 'seq')
- grad_signal: bfloat16 [4, 1024, 8192], P('batch', 'seq')
- grad_residues: float32 [8, 8192], replicated
- grad_rates: float32 [8, 512], replicated
Inputs may be any that keep to these rules, and one draw needn't show every extreme that they name: Each decay rate exp(log_rates) lies between 0.2 / 1024 and 1 / 30.
All inputs are finite; a program needn't handle non-finite values.
Results may differ from a plain program's by a relative error of at most 0.0012.
Values sent between devices are 32-bit elements; how exact they have to be, the bound alone decides.
A program may use at most 384 MiB of HBM per device.

v0:
```python
import jax
import jax.numpy as jnp
from jax import lax
from jax.sharding import PartitionSpec as P

M = 8
GROUP = 16
HIGHEST = lax.Precision.HIGHEST
HIGHER = lax.Precision.HIGH


def carried_in(shard, axis, combine, identity, reverse):
    peers, index = (lax.axis_size(axis), lax.axis_index(axis))
    everything = jax.tree.map(lambda part: lax.all_gather(part, axis), shard)
    start = jax.tree.map(
        lambda part, zero: jnp.broadcast_to(jnp.asarray(zero, part.dtype), part.shape),
        shard,
        identity,
    )

    def lap(k, before):
        at = peers - 1 - k if reverse else k
        reached = at > index if reverse else at < index
        new = combine(before, jax.tree.map(lambda part: part[at], everything))
        return jax.tree.map(lambda a, b: jnp.where(reached, a, b), new, before)

    return lax.fori_loop(0, peers, lap, start)


def depthwise(values, kernel, padding, precision):
    return lax.conv_general_dilated(
        values,
        kernel[:, None, :],
        (1,),
        [padding],
        dimension_numbers=("NWC", "WIO", "NWC"),
        feature_group_count=values.shape[2],
        precision=precision,
        preferred_element_type=jnp.float32,
    )


def local(signal, out_grad, residues, log_rates):
    batch_rows, length, channels = signal.shape
    groups = log_rates.shape[1]
    decay_rate = jnp.exp(log_rates)
    offsets = jnp.arange(length + 1, dtype=jnp.float32)
    powers = jnp.exp(-decay_rate[None] * offsets[:, None, None])
    res_group = residues.reshape(M, groups, GROUP)
    kernel = jnp.einsum("kmg,mgi->kgi", powers[:length], res_group, precision=HIGHEST).reshape(
        length, channels
    )
    inputs = signal.astype(jnp.float32)
    cotangent = out_grad.astype(jnp.float32)
    local_out = depthwise(inputs, kernel[::-1], (length - 1, 0), HIGHER)
    local_grad = depthwise(cotangent, kernel, (0, length - 1), HIGHER)
    weights = jnp.stack([powers[:length], offsets[:length, None, None] * powers[:length]])
    starts_table = jnp.stack([powers[:length], offsets[1:, None, None] * powers[1:]])
    input_group = inputs.reshape(batch_rows, length, groups, GROUP)
    grad_group = cotangent.reshape(batch_rows, length, groups, GROUP)
    end_states = jnp.einsum("jsmg,bsgi->jbmgi", weights[:, ::-1], input_group, precision=HIGHER)
    start_sums = jnp.einsum("jtmg,btgi->jbmgi", starts_table, grad_group, precision=HIGHER)
    local_state = end_states[0]
    local_moment = end_states[1]
    start_state = start_sums[0]
    weighted_start = start_sums[1]
    first_pole = powers[1][None, :, :, None]
    start_plain = first_pole * start_state
    empty_state = jnp.zeros_like(local_state)
    span = jnp.full((), float(length), jnp.float32)
    no_span = jnp.zeros((), jnp.float32)

    def join_forward(earlier, later):
        decay = jnp.exp(-decay_rate * later[0])[None, :, :, None]
        return (
            earlier[0] + later[0],
            decay * earlier[1] + later[1],
            decay * (earlier[2] + later[0] * earlier[1]) + later[2],
        )

    def join_backward(earlier, later):
        decay = jnp.exp(-decay_rate * later[0])[None, :, :, None]
        return (earlier[0] + later[0], decay * earlier[1] + later[1])

    forward_out = carried_in(
        (span, local_state, local_moment),
        "seq",
        join_forward,
        (no_span, empty_state, empty_state),
        False,
    )
    carry_state = forward_out[1]
    carry_moment = forward_out[2]
    backward_out = carried_in(
        (span, start_state), "seq", join_backward, (no_span, empty_state), True
    )
    adjoint = backward_out[1]
    out_extra = jnp.einsum(
        "tmg,bmgi->btgi", powers[1:], res_group[None] * carry_state, precision=HIGHEST
    ).reshape(batch_rows, length, channels)
    grad_extra = jnp.einsum(
        "tmg,bmgi->btgi", powers[1:][::-1], res_group[None] * adjoint, precision=HIGHEST
    ).reshape(batch_rows, length, channels)
    mixed = (local_out + out_extra).astype(jnp.bfloat16)
    grad_signal = (local_grad + grad_extra).astype(jnp.bfloat16)
    lag_values = jnp.swapaxes(out_grad, 0, 1).reshape(1, length, batch_rows * channels)
    lag_kernel = jnp.swapaxes(signal, 0, 1).reshape(length, batch_rows * channels)
    lagged = depthwise(lag_values, lag_kernel, (0, length - 1), None)
    lag_sums = jnp.sum(lagged.reshape(length, batch_rows, groups, GROUP), axis=1)
    lag_terms = jnp.einsum("jkmg,kgi->jmgi", weights, lag_sums, precision=HIGHEST)
    residue_part = lag_terms[0] + jnp.sum(carry_state * start_plain, axis=0)
    moment_part = lag_terms[1] + jnp.sum(
        carry_state * weighted_start + carry_moment * start_plain, axis=0
    )
    rate_part = -decay_rate * jnp.sum(res_group * moment_part, axis=2)
    norm_factor = 1.0 / (batch_rows * lax.axis_size("batch") * length * lax.axis_size("seq"))
    grad_residues, grad_rates = lax.psum(
        (residue_part.reshape(M, channels) * norm_factor, rate_part * norm_factor), ("seq", "batch")
    )
    return (mixed, grad_signal, grad_residues, grad_rates)


def solution(mesh):
    placed = (P("batch", "seq", None), P("batch", "seq", None), P(), P())
    return jax.shard_map(
        local,
        mesh=mesh,
        in_specs=placed,
        out_specs=(P("batch", "seq", None), P("batch", "seq", None), P(), P()),
        check_vma=False,
    )
```

profile of v0, /device:TPU:0, one launch (start us, length us, event | category | flops | bytes accessed | tf_op | source)
XLA Modules:
  0.0 764.3 jit_solution(8605537450636845793)
XLA Ops:
  15.2 7.2 rev.10
  36.5 6.5 fusion.9
  55.7 11.2 %fusion.23 = f32[512,128,16]{1,2,0:T(8,128)} fusion(f32[8,512,16]{2,1,0:T(8,128)S(1)} %reshape.109, f32[129,8,512]{0,1,2:T(8,128)} %copy-done), kind=kOutput, calls=%fused_computation.31 | convolution fusion | flops 100663296 | bytes 6553600 | tf_op jit(solution)/shard_map/kmg,mgi->kgi/dot_general | solution.py:50
  69.0 24.8 %all-reduce = f32[8]{0:T(128)} all-reduce(f32[8]{0:T(128)S(1)} %dynamic-update-slice), channel_id=1, replica_groups=mesh['seq'=8,'batch'=4] {'seq'}, use_global_device_ids=true, to_apply=%add | all-reduce | flops 8 | bytes 64
  93.7 62.1 %fusion.7 = f32[1,128,8192]{2,0,1:T(1,128)} fusion(bf16[128,1,8192]{2,0,1:T(8,128)(2,1)} %bitcast.133, bf16[1,128,8192]{2,1,0:T(8,128)(2,1)} %param.9), kind=kOutput, calls=%fused_computation.16 | convolution fusion | flops 135266304 | bytes 8388608 | tf_op jit(solution)/shard_map/conv_general_dilated | solution.py:31
  155.8 9.7 %copy.129 = f32[1,128,8192]{1,2,0:T(8,128)} copy(f32[1,128,8192]{2,0,1:T(1,128)} %fusion.7) | data formatting | bytes 8388608 | tf_op jit(solution)/shard_map/conv_general_dilated | solution.py:31
  165.5 12.2 %fusion.5 = f32[512,16,2,8]{1,3,2,0:T(8,128)} fusion(f32[128,512,16,1]{0,2,3,1:T(8,128)} %bitcast.123, f32[2,128,8,512]{1,2,3,0:T(8,128)} %get-tuple-element.514), kind=kOutput, calls=%fused_computation.14 | convolution fusion | flops 201326592 | bytes 8912896 | tf_op jit(solution)/shard_map/jkmg,kgi->jmgi/dot_general | solution.py:110
  186.0 9.6 %copy.119 = f32[128,1,8192]{2,1,0:T(1,128)} copy(f32[128,1,8192]{0,2,1:T(8,128)} %bitcast.121) | data formatting | bytes 8388608 | tf_op jit(solution)/shard_map/broadcast_in_dim;reshape | solution.py:33
  201.2 32.7 %rev.9 = f32[128,8192]{1,0:T(8,128)} reverse(f32[128,8192]{1,0:T(8,128)} %copy.108), dimensions={0} | reverse | bytes 8388608 | tf_op jit(solution)/shard_map/rev | solution.py:55
  233.9 6.6 broadcast_in_dim.16
  240.5 22.5 %all-gather.4.cloned.1.call-done = f32[8,1,8,512,16]{4,2,0,3,1:T(8,128)} async-done(((f32[1,1,8,512,16]{4,2,0,3,1:T(8,128)}), f32[8,1,8,512,16]{4,2,0,3,1:T(8,128)}) %all-gather.4.cloned.1.call-update) | async-done | bytes 2097168 | tf_op jit(solution)/shard_map/all_gather | solution.py:14
  263.0 10.3 %copy.113 = f32[8,1,8,512,16]{3,4,2,1,0:T(8,128)S(1)} copy(f32[8,1,8,512,16]{4,2,0,3,1:T(8,128)} %all-gather.4.cloned.1.call-done) | data formatting | bytes 4194304
  273.4 217.2 %all-gather.6.cloned.1.call-done = f32[8,1,8,512,16]{4,2,0,3,1:T(8,128)} async-done(((f32[1,1,8,512,16]{4,2,0,3,1:T(8,128)}), f32[8,1,8,512,16]{4,2,0,3,1:T(8,128)}) %all-gather.6.cloned.1.call-update) | async-done | bytes 2097168 | tf_op jit(solution)/shard_map/all_gather | solution.py:14
  490.6 10.9 %copy.114 = f32[8,1,8,512,16]{3,4,2,1,0:T(8,128)} copy(f32[8,1,8,512,16]{4,2,0,3,1:T(8,128)} %all-gather.6.cloned.1.call-done) | data formatting | bytes 4194304
  501.5 25.2 %while.34 = (s32[]{:T(128)}, f32[1,8,512,16]{2,3,1,0:T(8,128)S(1)}, f32[1,8,512,16]{2,3,1,0:T(8,128)S(1)}, s32[]{:T(128)}, f32[8]{0:T(128)S(1)}, /*index=5*/f32[...) while((s32[]{:T(128)}, f32[1,8,512,16]{2,3,1,0:T(8,128)S(1)}, ...), condition=%wide.region_1.2_spmd.clone, body=%wide.region_0.1_spmd.clone.sunk | while | flops 659460 | bytes 1622161 | solution.py:27
  540.0 19.6 %while.35 = (s32[]{:T(128)}, f32[1,8,512,16]{2,3,1,0:T(8,128)S(1)}, s32[]{:T(128)}, f32[8]{0:T(128)S(1)}, f32[1,8,512,1]{2,1,3,0:T(8,128)S(1)}, /*index=5*/f32[8...) while((s32[]{:T(128)}, f32[1,8,512,16]{2,3,1,0:T(8,128)S(1)}, s32[]{:T(128)}, ...), condition=%wide.region_3.4_spmd.clone, body=%wide.region_2.3_spmd.clone.sunk | while | flops 266248 | bytes 835771 | solution.py:27
  565.6 10.0 %fusion.19 = f32[512,16,128]{2,1,0:T(8,128)} fusion(f32[128,8,512]{0,1,2:T(8,128)S(1)} %copy-done.7, f32[8,512,16]{2,1,0:T(8,128)S(1)} %get-tuple-element.511), kind=kOutput, calls=%fused_computation.27 | convolution fusion | flops 100663296 | bytes 6553600 | tf_op jit(solution)/shard_map/tmg,bmgi->btgi/dot_general | solution.py:101
  575.6 9.8 %copy.126 = f32[1,128,8192]{2,0,1:T(1,128)} copy(f32[1,128,8192]{1,2,0:T(8,128)} %bitcast.124) | data formatting | bytes 8388608 | tf_op jit(solution)/shard_map/reshape | solution.py:103
  585.5 12.4 %fusion.21 = f32[512,16,128]{2,1,0:T(8,128)} fusion(f32[8,512,16]{2,1,0:T(8,128)S(1)} %copy-done.6, f32[129,8,512]{0,1,2:T(8,128)} %copy-done), kind=kOutput, calls=%fused_computation.29 | convolution fusion | flops 100663296 | bytes 6553600 | tf_op jit(solution)/shard_map/tmg,bmgi->btgi/dot_general | solution.py:98
  597.8 9.8 %copy.117 = f32[1,128,8192]{2,0,1:T(1,128)} copy(f32[1,128,8192]{1,2,0:T(8,128)} %bitcast.125) | data formatting | bytes 8388608 | tf_op jit(solution)/shard_map/reshape | solution.py:100
  607.7 47.8 %fusion.3 = bf16[1,128,8192]{2,0,1:T(2,128)(2,1)} fusion(f32[1,128,8192]{2,0,1:T(1,128)} %copy.126, f32[128,1,8192]{2,1,0:T(1,128)} %copy.119, bf16[1,128,8192]{2,1,0:T(8,128)(2,1)S(1)} %copy-done.16), kind=kOutput, calls=%fused_computation.9 | convolution fusion | flops 407896064 | bytes 12582912 | tf_op jit(solution)/shard_map/conv_general_dilated | solution.py:31
  655.5 46.6 %fusion.4 = bf16[1,128,8192]{2,0,1:T(2,128)(2,1)} fusion(f32[1,128,8192]{2,0,1:T(1,128)S(1)} %copy-done.12, f32[128,1,8192]{2,1,0:T(1,128)S(1)} %copy-done.11, bf16[1,128,8192]{2,1,0:T(8,128)(2,1)S(1)} %copy-done.17), kind=kOutput, calls=%fused_computation.11 | convolution fusion | flops 407896064 | bytes 12582912 | tf_op jit(solution)/shard_map/conv_general_dilated | solution.py:31
  702.2 43.2 %psum.15 = f32[8,512]{0,1:T(8,128)S(1)} all-reduce(f32[8,512]{0,1:T(8,128)S(1)} %multiply_multiply_fusion), channel_id=1, replica_groups=mesh['seq'=8,'batch'=4] {'seq','batch'}, use_global_device_ids=true, to_apply=%region_6.7 | all-reduce | flops 4096 | bytes 32768 | tf_op jit(solution)/shard_map/psum | solution.py:117
  746.1 5.9 copy.137
  (149 shorter events, 120.0 us)
Async XLA Ops:
  7.2 255.8 %all-gather.4.cloned.1.call-start = ((), (), s32[]{:S(2)}) async-start(), calls=%async_computation | async-start | bytes 18874368 | tf_op jit(solution)/shard_map/all_gather | solution.py:14
  32.5 458.1 %all-gather.6.cloned.1.call-start = ((), (), s32[]{:S(2)}) async-start(), calls=%async_computation.1 | async-start | bytes 18874368 | tf_op jit(solution)/shard_map/all_gather | solution.py:14
  33.3 506.8 %all-gather.8.cloned.1.call-start = ((), (), s32[]{:S(2)}) async-start(), calls=%async_computation.2 | async-start | bytes 2359296 | tf_op jit(solution)/shard_map/all_gather | solution.py:14
  43.0 8.6 %copy-start.19 = (f32[8,8192]{1,0:T(8,128)S(1)}, f32[8,8192]{1,0:T(8,128)}, u32[]{:S(2)}) copy-start(f32[8,8192]{1,0:T(8,128)} %param.10) | copy-start | bytes 786436
  46.6 5.1 copy-start.8
  47.4 708.2 %all-reduce.3.cloned.1.call-start = ((), (), s32[]{:S(2)}) async-start(), calls=%async_computation.3 | async-start | bytes 524288 | tf_op jit(solution)/shard_map/psum | solution.py:117
  55.7 11.2 %copy-start.23 = (u32[32]{0:T(128)S(1)}, u32[32]{0:T(128)}, u32[]{:S(2)}) copy-start(u32[32]{0:T(128)} %constant.98) | copy-start | bytes 388
  177.6 5.9 copy-start.5
  273.3 228.2 %copy-start.1 = (f32[1,8,512,16]{2,3,1,0:T(8,128)S(1)}, f32[1,8,512,16]{2,3,1,0:T(8,128)}, u32[]{:S(2)}) copy-start(f32[1,8,512,16]{2,3,1,0:T(8,128)} %custom-call) | copy-start | bytes 786436
  273.3 228.2 %copy-start.2 = (f32[1,8,512,16]{2,3,1,0:T(8,128)S(1)}, f32[1,8,512,16]{2,3,1,0:T(8,128)}, u32[]{:S(2)}) copy-start(f32[1,8,512,16]{2,3,1,0:T(8,128)} %custom-call.1) | copy-start | bytes 786436
  273.3 228.1 %copy-start.18 = (f32[1,8,512,1]{2,1,3,0:T(8,128)S(1)}, f32[1,8,512,1]{2,1,3,0:T(8,128)}, u32[]{:S(2)}) copy-start(f32[1,8,512,1]{2,1,3,0:T(8,128)} %copy.112) | copy-start | bytes 49156
  273.3 228.1 %copy-start.22 = (f32[8]{0:T(128)S(1)}, f32[8]{0:T(128)}, u32[]{:S(2)}) copy-start(f32[8]{0:T(128)} %all-reduce) | copy-start | bytes 100
  501.5 27.2 %copy-start.9 = (f32[512,2,8,16]{0,3,2,1:T(8,128)S(1)}, f32[512,2,8,16]{0,3,2,1:T(8,128)}, u32[]{:S(2)}) copy-start(f32[512,2,8,16]{0,3,2,1:T(8,128)} %copy-done.8) | copy-start | bytes 1572868
  501.5 27.2 %copy-start.20 = (f32[8,512,16]{1,2,0:T(8,128)S(1)}, f32[8,512,16]{1,2,0:T(8,128)}, u32[]{:S(2)}) copy-start(f32[8,512,16]{1,2,0:T(8,128)} %copy.134) | copy-start | bytes 786436
  528.7 11.3 %copy-start.3 = (f32[1,8,512,16]{2,3,1,0:T(8,128)S(1)}, f32[1,8,512,16]{2,3,1,0:T(8,128)}, u32[]{:S(2)}) copy-start(f32[1,8,512,16]{2,3,1,0:T(8,128)} %custom-call.2) | copy-start | bytes 786436
  532.7 28.8 %copy-start.4 = (f32[1,8,512,16]{3,2,1,0:T(8,128)S(1)}, f32[1,8,512,16]{3,2,1,0:T(8,128)}, u32[]{:S(2)}) copy-start(f32[1,8,512,16]{3,2,1,0:T(8,128)} %broadcast_in_dim_reshape.7) | copy-start | bytes 786436
  575.6 9.8 %copy-start.6 = (f32[8,512,16]{2,1,0:T(8,128)S(1)}, f32[8,512,16]{2,1,0:T(8,128)}, u32[]{:S(2)}) copy-start(f32[8,512,16]{2,1,0:T(8,128)} %get-tuple-element.512) | copy-start | bytes 786436
  597.8 9.8 %copy-start.16 = (bf16[1,128,8192]{2,1,0:T(8,128)(2,1)S(1)}, bf16[1,128,8192]{2,1,0:T(8,128)(2,1)}, u32[]{:S(2)}) copy-start(bf16[1,128,8192]{2,1,0:T(8,128)(2,1)} %param.9) | copy-start | bytes 6291460
  607.7 47.8 %copy-start.11 = (f32[128,1,8192]{2,1,0:T(1,128)S(1)}, f32[128,1,8192]{2,1,0:T(1,128)}, u32[]{:S(2)}) copy-start(f32[128,1,8192]{2,1,0:T(1,128)} %broadcast_in_dim.16) | copy-start | bytes 12582916
  607.7 47.8 %copy-start.12 = (f32[1,128,8192]{2,0,1:T(1,128)S(1)}, f32[1,128,8192]{2,0,1:T(1,128)}, u32[]{:S(2)}) copy-start(f32[1,128,8192]{2,0,1:T(1,128)} %copy.117) | copy-start | bytes 12582916
  607.7 47.8 %copy-start.17 = (bf16[1,128,8192]{2,1,0:T(8,128)(2,1)S(1)}, bf16[1,128,8192]{2,1,0:T(8,128)(2,1)}, u32[]{:S(2)}) copy-start(bf16[1,128,8192]{2,1,0:T(8,128)(2,1)} %param.8) | copy-start | bytes 6291460
  655.5 46.6 %copy-start.14 = (f32[8,512]{0,1:T(8,128)S(1)}, f32[8,512]{0,1:T(8,128)}, u32[]{:S(2)}) copy-start(f32[8,512]{0,1:T(8,128)} %copy-done.13) | copy-start | bytes 49156
  655.5 46.6 %copy-start.21 = (f32[8,512]{0,1:T(8,128)S(1)}, f32[8,512]{0,1:T(8,128)}, u32[]{:S(2)}) copy-start(f32[8,512]{0,1:T(8,128)} %copy.142) | copy-start | bytes 49156
  746.1 6.0 copy-start.10
  (4 other events, 14.1 us)
Sparse Core Ops, SparseCore 0:
  32.6 230.3 all-gather.3
  265.1 225.4 all-gather.5
  492.7 47.2 all-gather.7
  545.4 125.0 all-reduce.2
where the time goes:
time: 776 us; the launch traced here: 764 us
  waiting for transfers between devices  244 us (31%)
  matrix products  213 us (27%)
  local copies, waits for them, and re-layouts  176 us (23%)
  blocking collectives  68 us (9%)
  other arithmetic  47 us (6%)
  between operations  14.6 us (2%)
    all_gather x3, waiting for transfers between devices, carried_in(): everything = jax.tree.map(lambda part: lax.all_gather(part, axis), shard)  243 us
    conv_general_dilated x3, matrix products, depthwise(): lax.conv_general_dilated(values, kernel[:, None, :], (1,), [padding], dim...  156 us
    psum x1, blocking collectives, local(): lax.psum((residue_part.reshape(M, channels) * norm_factor, rate_part * no...  43.2 us
    unnamed x61, local copies, waits for them, and re-layouts  42.5 us
    rev x1, local copies, waits for them, and re-layouts, local(): local_out = depthwise(inputs, kernel[::-1], (length - 1, 0), HIGHER)  32.7 us
    unnamed x1, blocking collectives  24.8 us
    select_n x16, other arithmetic, lap(): return jax.tree.map(lambda a, b: jnp.where(reached, a, b), new, before)  24.2 us
  transfers between devices with their start and end apart: 4, of which 3 were waited for; matrix products, arithmetic and copies ran while one was open for 54% of the time, Pallas kernels for 0%

commit v1 on v0

--- a/solution.py
+++ b/solution.py
@@ -115,7 +115,8 @@
     rate_part = -decay_rate * jnp.sum(res_group * moment_part, axis=2)
     norm_factor = 1.0 / (batch_rows * lax.axis_size("batch") * length * lax.axis_size("seq"))
     grad_residues, grad_rates = lax.psum(
-        (residue_part.reshape(M, channels) * norm_factor, rate_part * norm_factor), ("seq", "batch")
+        lax.psum((residue_part.reshape(M, channels) * norm_factor, rate_part * norm_factor), "seq"),
+        "batch",
     )
     return (mixed, grad_signal, grad_residues, grad_rates)
 

time: 776 us -> 784 us (1.010)
    psum x0 -> x1, blocking collectives: none -> 12.8 us  [local(): lax.psum(lax.psum((residue_part.reshape(M, channels) * norm_factor, rate_...]
    unnamed x61 -> x73, local copies, waits for them, and re-layouts: 42.5 us -> 41.9 us
  transfers between devices with their start and end apart: 4 -> 5, of which waited for: 3 -> 3; matrix products, arithmetic and copies ran while one was open for 54% -> 53% of each run, Pallas kernels for 0% -> 0%
where the time goes in v1:
time: 784 us; the launch traced here: 772 us
  waiting for transfers between devices  245 us (31%)
  matrix products  213 us (27%)
  local copies, waits for them, and re-layouts  176 us (22%)
  blocking collectives  75.4 us (10%)
  other arithmetic  47 us (6%)
  between operations  14.7 us (2%)
    all_gather x3, waiting for transfers between devices, carried_in(): everything = jax.tree.map(lambda part: lax.all_gather(part, axis), shard)  244 us
    conv_general_dilated x3, matrix products, depthwise(): lax.conv_general_dilated(values, kernel[:, None, :], (1,), [padding], dim...  157 us
    unnamed x73, local copies, waits for them, and re-layouts  41.9 us
    psum x1, blocking collectives, local(): lax.psum((residue_part.reshape(M, channels) * norm_factor, rate_part * no...  37.8 us
    rev x1, local copies, waits for them, and re-layouts, local(): local_out = depthwise(inputs, kernel[::-1], (length - 1, 0), HIGHER)  32.7 us
    unnamed x1, blocking collectives  24.7 us
    select_n x16, other arithmetic, lap(): return jax.tree.map(lambda a, b: jnp.where(reached, a, b), new, before)  24.2 us
  transfers between devices with their start and end apart: 5, of which 3 were waited for; matrix products, arithmetic and copies ran while one was open for 53% of the time, Pallas kernels for 0%

profile of v1, /device:TPU:0, one launch (start us, length us, event | category | flops | bytes accessed | tf_op | source)
XLA Modules:
  0.0 772.4 jit_solution(12606575729807733718)
XLA Ops:
  15.2 7.2 rev.10
  36.5 6.5 fusion.9
  55.7 11.2 %fusion.23 = f32[512,128,16]{1,2,0:T(8,128)} fusion(f32[8,512,16]{2,1,0:T(8,128)S(1)} %reshape.109, f32[129,8,512]{0,1,2:T(8,128)} %copy-done), kind=kOutput, calls=%fused_computation.31 | convolution fusion | flops 100663296 | bytes 6553600 | tf_op jit(solution)/shard_map/kmg,mgi->kgi/dot_general | solution.py:50
  69.0 24.7 %all-reduce = f32[8]{0:T(128)} all-reduce(f32[8]{0:T(128)S(1)} %dynamic-update-slice), channel_id=1, replica_groups=mesh['seq'=8,'batch'=4] {'seq'}, use_global_device_ids=true, to_apply=%add | all-reduce | flops 8 | bytes 64
  93.6 62.1 %fusion.7 = f32[1,128,8192]{2,0,1:T(1,128)} fusion(bf16[128,1,8192]{2,0,1:T(8,128)(2,1)} %bitcast.133, bf16[1,128,8192]{2,1,0:T(8,128)(2,1)} %param.9), kind=kOutput, calls=%fused_computation.16 | convolution fusion | flops 135266304 | bytes 8388608 | tf_op jit(solution)/shard_map/conv_general_dilated | solution.py:31
  155.7 9.7 %copy.129 = f32[1,128,8192]{1,2,0:T(8,128)} copy(f32[1,128,8192]{2,0,1:T(1,128)} %fusion.7) | data formatting | bytes 8388608 | tf_op jit(solution)/shard_map/conv_general_dilated | solution.py:31
  165.4 12.2 %fusion.5 = f32[512,16,2,8]{1,3,2,0:T(8,128)} fusion(f32[128,512,16,1]{0,2,3,1:T(8,128)} %bitcast.123, f32[2,128,8,512]{1,2,3,0:T(8,128)} %get-tuple-element.514), kind=kOutput, calls=%fused_computation.14 | convolution fusion | flops 201326592 | bytes 8912896 | tf_op jit(solution)/shard_map/jkmg,kgi->jmgi/dot_general | solution.py:110
  185.8 9.7 %copy.119 = f32[128,1,8192]{2,1,0:T(1,128)} copy(f32[128,1,8192]{0,2,1:T(8,128)} %bitcast.121) | data formatting | bytes 8388608 | tf_op jit(solution)/shard_map/broadcast_in_dim;reshape | solution.py:33
  201.1 32.7 %rev.9 = f32[128,8192]{1,0:T(8,128)} reverse(f32[128,8192]{1,0:T(8,128)} %copy.108), dimensions={0} | reverse | bytes 8388608 | tf_op jit(solution)/shard_map/rev | solution.py:55
  233.8 6.6 broadcast_in_dim.16
  240.4 22.7 %all-gather.4.cloned.1.call-done = f32[8,1,8,512,16]{4,2,0,3,1:T(8,128)} async-done(((f32[1,1,8,512,16]{4,2,0,3,1:T(8,128)}), f32[8,1,8,512,16]{4,2,0,3,1:T(8,128)}) %all-gather.4.cloned.1.call-update) | async-done | bytes 2097168 | tf_op jit(solution)/shard_map/all_gather | solution.py:14
  263.0 10.3 %copy.113 = f32[8,1,8,512,16]{3,4,2,1,0:T(8,128)S(1)} copy(f32[8,1,8,512,16]{4,2,0,3,1:T(8,128)} %all-gather.4.cloned.1.call-done) | data formatting | bytes 4194304
  273.4 217.2 %all-gather.6.cloned.1.call-done = f32[8,1,8,512,16]{4,2,0,3,1:T(8,128)} async-done(((f32[1,1,8,512,16]{4,2,0,3,1:T(8,128)}), f32[8,1,8,512,16]{4,2,0,3,1:T(8,128)}) %all-gather.6.cloned.1.call-update) | async-done | bytes 2097168 | tf_op jit(solution)/shard_map/all_gather | solution.py:14
  490.6 10.9 %copy.114 = f32[8,1,8,512,16]{3,4,2,1,0:T(8,128)} copy(f32[8,1,8,512,16]{4,2,0,3,1:T(8,128)} %all-gather.6.cloned.1.call-done) | data formatting | bytes 4194304
  501.5 25.0 %while.34 = (s32[]{:T(128)}, f32[1,8,512,16]{2,3,1,0:T(8,128)S(1)}, f32[1,8,512,16]{2,3,1,0:T(8,128)S(1)}, s32[]{:T(128)}, f32[8]{0:T(128)S(1)}, /*index=5*/f32[...) while((s32[]{:T(128)}, f32[1,8,512,16]{2,3,1,0:T(8,128)S(1)}, ...), condition=%wide.region_1.2_spmd.clone, body=%wide.region_0.1_spmd.clone.sunk | while | flops 659460 | bytes 1622161 | solution.py:27
  540.0 19.8 %while.35 = (s32[]{:T(128)}, f32[1,8,512,16]{2,3,1,0:T(8,128)S(1)}, s32[]{:T(128)}, f32[8]{0:T(128)S(1)}, f32[1,8,512,1]{2,1,3,0:T(8,128)S(1)}, /*index=5*/f32[8...) while((s32[]{:T(128)}, f32[1,8,512,16]{2,3,1,0:T(8,128)S(1)}, s32[]{:T(128)}, ...), condition=%wide.region_3.4_spmd.clone, body=%wide.region_2.3_spmd.clone.sunk | while | flops 266248 | bytes 835771 | solution.py:27
  565.8 10.0 %fusion.19 = f32[512,16,128]{2,1,0:T(8,128)} fusion(f32[128,8,512]{0,1,2:T(8,128)S(1)} %copy-done.11, f32[8,512,16]{2,1,0:T(8,128)S(1)} %get-tuple-element.511), kind=kOutput, calls=%fused_computation.27 | convolution fusion | flops 100663296 | bytes 6553600 | tf_op jit(solution)/shard_map/tmg,bmgi->btgi/dot_general | solution.py:101
  575.8 9.8 %copy.126 = f32[1,128,8192]{2,0,1:T(1,128)} copy(f32[1,128,8192]{1,2,0:T(8,128)} %bitcast.124) | data formatting | bytes 8388608 | tf_op jit(solution)/shard_map/reshape | solution.py:103
  585.6 12.1 %fusion.21 = f32[512,16,128]{2,1,0:T(8,128)} fusion(f32[8,512,16]{2,1,0:T(8,128)S(1)} %copy-done.10, f32[129,8,512]{0,1,2:T(8,128)} %copy-done), kind=kOutput, calls=%fused_computation.29 | convolution fusion | flops 100663296 | bytes 6553600 | tf_op jit(solution)/shard_map/tmg,bmgi->btgi/dot_general | solution.py:98
  597.7 9.8 %copy.117 = f32[1,128,8192]{2,0,1:T(1,128)} copy(f32[1,128,8192]{1,2,0:T(8,128)} %bitcast.125) | data formatting | bytes 8388608 | tf_op jit(solution)/shard_map/reshape | solution.py:100
  607.6 47.8 %fusion.3 = bf16[1,128,8192]{2,0,1:T(2,128)(2,1)} fusion(f32[1,128,8192]{2,0,1:T(1,128)} %copy.126, f32[128,1,8192]{2,1,0:T(1,128)} %copy.119, bf16[1,128,8192]{2,1,0:T(8,128)(2,1)S(1)} %copy-done.21), kind=kOutput, calls=%fused_computation.9 | convolution fusion | flops 407896064 | bytes 12582912 | tf_op jit(solution)/shard_map/conv_general_dilated | solution.py:31
  655.4 46.8 %fusion.4 = bf16[1,128,8192]{2,0,1:T(2,128)(2,1)} fusion(f32[1,128,8192]{2,0,1:T(1,128)S(1)} %copy-done.17, f32[128,1,8192]{2,1,0:T(1,128)S(1)} %copy-done.16, bf16[1,128,8192]{2,1,0:T(8,128)(2,1)S(1)} %copy-done.22), kind=kOutput, calls=%fused_computation.11 | convolution fusion | flops 407896064 | bytes 12582912 | tf_op jit(solution)/shard_map/conv_general_dilated | solution.py:31
  702.8 37.8 %psum.30 = f32[8,512]{0,1:T(8,128)S(1)} all-reduce(f32[8,512]{0,1:T(8,128)S(1)} %multiply_multiply_fusion), channel_id=1, replica_groups=mesh['seq'=8,'batch'=4] {'seq'}, use_global_device_ids=true, to_apply=%region_7.8 | all-reduce | flops 4096 | bytes 32768 | tf_op jit(solution)/shard_map/psum | solution.py:118
  740.6 12.8 %psum.31 = f32[8,512]{0,1:T(8,128)S(1)} all-reduce(f32[8,512]{0,1:T(8,128)S(1)} %psum.30), channel_id=1, replica_groups=mesh['seq'=8,'batch'=4] {'batch'}, use_global_device_ids=true, to_apply=%region_8.9 | all-reduce | flops 4096 | bytes 32768 | tf_op jit(solution)/shard_map/psum | solution.py:117
  (165 shorter events, 126.5 us)
Async XLA Ops:
  7.2 255.9 %all-gather.4.cloned.1.call-start = ((), (), s32[]{:S(2)}) async-start(), calls=%async_computation | async-start | bytes 18874368 | tf_op jit(solution)/shard_map/all_gather | solution.py:14
  32.5 458.1 %all-gather.6.cloned.1.call-start = ((), (), s32[]{:S(2)}) async-start(), calls=%async_computation.1 | async-start | bytes 18874368 | tf_op jit(solution)/shard_map/all_gather | solution.py:14
  33.3 506.8 %all-gather.8.cloned.1.call-start = ((), (), s32[]{:S(2)}) async-start(), calls=%async_computation.2 | async-start | bytes 2359296 | tf_op jit(solution)/shard_map/all_gather | solution.py:14
  47.4 655.3 %all-reduce.4.cloned.1.call-start = ((), (), s32[]{:S(2)}) async-start(), calls=%async_computation.3 | async-start | bytes 524288 | tf_op jit(solution)/shard_map/psum | solution.py:118
  55.7 11.2 %copy-start.29 = (u32[32]{0:T(128)S(1)}, u32[32]{0:T(128)}, u32[]{:S(2)}) copy-start(u32[32]{0:T(128)} %constant.98) | copy-start | bytes 388
  183.4 345.1 %copy-start.26 = (f32[1,8,512]{2,1,0:T(8,128)}, f32[1,8,512]{2,1,0:T(8,128)S(1)}, u32[]{:S(2)}) copy-start(f32[1,8,512]{2,1,0:T(8,128)S(1)} %copy.132) | copy-start | bytes 49156
  273.3 228.2 %copy-start.1 = (f32[1,8,512,16]{2,3,1,0:T(8,128)S(1)}, f32[1,8,512,16]{2,3,1,0:T(8,128)}, u32[]{:S(2)}) copy-start(f32[1,8,512,16]{2,3,1,0:T(8,128)} %custom-call) | copy-start | bytes 786436
  273.3 228.2 %copy-start.4 = (f32[1,8,512,16]{2,3,1,0:T(8,128)S(1)}, f32[1,8,512,16]{2,3,1,0:T(8,128)}, u32[]{:S(2)}) copy-start(f32[1,8,512,16]{2,3,1,0:T(8,128)} %custom-call.1) | copy-start | bytes 786436
  273.4 228.1 %copy-start.23 = (f32[1,8,512,1]{2,1,3,0:T(8,128)S(1)}, f32[1,8,512,1]{2,1,3,0:T(8,128)}, u32[]{:S(2)}) copy-start(f32[1,8,512,1]{2,1,3,0:T(8,128)} %copy.112) | copy-start | bytes 49156
  273.4 228.1 %copy-start.28 = (f32[8]{0:T(128)S(1)}, f32[8]{0:T(128)}, u32[]{:S(2)}) copy-start(f32[8]{0:T(128)} %all-reduce) | copy-start | bytes 100
  501.5 27.0 %copy-start.13 = (f32[512,2,8,16]{0,3,2,1:T(8,128)S(1)}, f32[512,2,8,16]{0,3,2,1:T(8,128)}, u32[]{:S(2)}) copy-start(f32[512,2,8,16]{0,3,2,1:T(8,128)} %copy-done.12) | copy-start | bytes 1572868
  526.5 13.5 %copy-start.7 = (f32[1,8,512,16]{2,3,1,0:T(8,128)S(1)}, f32[1,8,512,16]{2,3,1,0:T(8,128)}, u32[]{:S(2)}) copy-start(f32[1,8,512,16]{2,3,1,0:T(8,128)} %custom-call.2) | copy-start | bytes 786436
  531.5 30.3 %copy-start.8 = (f32[1,8,512,16]{3,2,1,0:T(8,128)S(1)}, f32[1,8,512,16]{3,2,1,0:T(8,128)}, u32[]{:S(2)}) copy-start(f32[1,8,512,16]{3,2,1,0:T(8,128)} %broadcast_in_dim_reshape.7) | copy-start | bytes 786436
  535.5 228.2 %all-reduce.6.cloned.1.call-start = ((), (), s32[]{:S(2)}) async-start(), calls=%async_computation.4 | async-start | bytes 524288 | tf_op jit(solution)/shard_map/psum | solution.py:117
  607.6 47.8 %copy-start.16 = (f32[128,1,8192]{2,1,0:T(1,128)S(1)}, f32[128,1,8192]{2,1,0:T(1,128)}, u32[]{:S(2)}) copy-start(f32[128,1,8192]{2,1,0:T(1,128)} %broadcast_in_dim.16) | copy-start | bytes 12582916
  607.6 47.8 %copy-start.17 = (f32[1,128,8192]{2,0,1:T(1,128)S(1)}, f32[1,128,8192]{2,0,1:T(1,128)}, u32[]{:S(2)}) copy-start(f32[1,128,8192]{2,0,1:T(1,128)} %copy.117) | copy-start | bytes 12582916
  607.6 47.8 %copy-start.22 = (bf16[1,128,8192]{2,1,0:T(8,128)(2,1)S(1)}, bf16[1,128,8192]{2,1,0:T(8,128)(2,1)}, u32[]{:S(2)}) copy-start(bf16[1,128,8192]{2,1,0:T(8,128)(2,1)} %param.8) | copy-start | bytes 6291460
  655.4 46.9 %copy-start.3 = (f32[1,8,512,16]{2,3,1,0:T(8,128)S(1)}, f32[1,8,512,16]{2,3,1,0:T(8,128)}, u32[]{:S(2)}) copy-start(f32[1,8,512,16]{2,3,1,0:T(8,128)} %copy-done.2) | copy-start | bytes 786436
  655.4 46.9 %copy-start.6 = (f32[1,8,512,16]{2,3,1,0:T(8,128)S(1)}, f32[1,8,512,16]{2,3,1,0:T(8,128)}, u32[]{:S(2)}) copy-start(f32[1,8,512,16]{2,3,1,0:T(8,128)} %copy-done.5) | copy-start | bytes 786436
  655.4 46.9 %copy-start.14 = (f32[512,2,8,16]{0,3,2,1:T(8,128)S(1)}, f32[512,2,8,16]{0,3,2,1:T(8,128)}, u32[]{:S(2)}) copy-start(f32[512,2,8,16]{0,3,2,1:T(8,128)} %copy-done.12) | copy-start | bytes 1572868
  655.4 46.9 %copy-start.20 = (f32[512,16,2,8]{0,1,3,2:T(8,128)S(1)}, f32[512,16,2,8]{0,1,3,2:T(8,128)}, u32[]{:S(2)}) copy-start(f32[512,16,2,8]{0,1,3,2:T(8,128)} %copy.131) | copy-start | bytes 1572868
  655.4 46.9 %copy-start.25 = (f32[8,512,16]{1,2,0:T(8,128)S(1)}, f32[8,512,16]{1,2,0:T(8,128)}, u32[]{:S(2)}) copy-start(f32[8,512,16]{1,2,0:T(8,128)} %copy.134) | copy-start | bytes 786436
  655.4 46.9 %copy-start.27 = (f32[1,8,512]{2,1,0:T(8,128)S(1)}, f32[1,8,512]{2,1,0:T(8,128)}, u32[]{:S(2)}) copy-start(f32[1,8,512]{2,1,0:T(8,128)} %copy-done.26) | copy-start | bytes 49156
  655.4 47.3 %copy-start.19 = (f32[8,512]{0,1:T(8,128)S(1)}, f32[8,512]{0,1:T(8,128)}, u32[]{:S(2)}) copy-start(f32[8,512]{0,1:T(8,128)} %copy-done.18) | copy-start | bytes 49156
  (11 other events, 73.5 us)
Sparse Core Ops, SparseCore 0:
  32.6 230.3 all-gather.3
  265.1 225.4 all-gather.5
  492.7 47.2 all-gather.7
  543.2 69.5 all-reduce.3
  702.8 30.7 all-reduce.5
